TPU v7x, 512 devices: a whole 4x4x16 slice. The times are simulated.
512 devices in a mesh: basis: 16 (over x, y), docs: 32 (over z, core).
Axes of the slice: x: 4, y: 4, z: 16, core: 2. Of those that a mesh axis runs over, the one named last changes fastest.
Arguments:
- eig_in: bfloat16 [28672, 28672], P('basis', 'docs'), may hold values from -0.03125 to 0.03125
- eig_out: bfloat16 [8192, 8192], P('basis', 'docs'), may hold values from -0.0625 to 0.0625
- eigvals: bfloat16 [8192, 28672], P('basis', 'docs'), may hold values from 0.0025 to 3.6
- out_factors: bfloat16 [8192, 256], P('docs'), may hold values from -1.1953125 to 1.1953125
- in_factors: bfloat16 [28672, 256], P(('basis', 'docs')), may hold values from -1.1953125 to 1.1953125
- test_matrix: bfloat16 [28672, 32], P('docs'), may hold values from -0.03125 to 0.03125
- activations: bfloat16 [4096, 28672], P('docs', 'basis'), may hold values from -6 to 6
- gradients: bfloat16 [4096, 8192], P('docs', 'basis'), may hold values from -0.00059890747 to 0.00059890747
- doc_lengths: int32 [128], replicated, may hold values from 1 to 96, 4096 in all
Outputs:
- scores: float32 [4096, 4], P('docs')
- doc_influence: float32 [128, 4], replicated
Inputs may be any that keep to these rules, and one draw needn't show every extreme that they name: `doc_lengths`: the documents lie end to end in token order and their lengths sum to 4096.
All inputs are finite; a program needn't handle non-finite values.
Results may differ from a plain program's by a relative error of at most 0.0085.
Values may be sent and summed in bfloat16 or wider, within the bound.
A program may use at most 64 MiB of HBM per device.

v0:
```python
import jax
import jax.numpy as jnp
from jax import lax
from jax.sharding import PartitionSpec as P

QUERIES = 4
LQ = 64
RANK = 32
damping = 0.1
highest = lax.Precision.HIGHEST


def local(
    eig_in,
    eig_out,
    eigvals,
    out_factors,
    in_factors,
    test_matrix,
    activations,
    gradients,
    doc_lengths,
):
    cols_in = eig_in.shape[1]
    rows_out = eig_out.shape[0]
    cols_out = eig_out.shape[1]
    tok_count = activations.shape[0]
    partial_in = lax.dot_general(
        eig_in,
        lax.all_gather(in_factors, "docs", axis=0, tiled=True),
        (((0,), (0,)), ((), ())),
        preferred_element_type=jnp.float32,
    )
    partial_out = jnp.dot(eig_out, out_factors, preferred_element_type=jnp.float32)
    rot_in = lax.psum(partial_in, "basis").astype(jnp.bfloat16)
    rot_out = lax.psum(partial_out, "docs").astype(jnp.bfloat16)
    weight = 1.0 / (eigvals.astype(jnp.float32) + damping)
    moment = (
        jnp.einsum(
            "iqs,jqs->qij",
            rot_out.reshape(rows_out, QUERIES, LQ),
            rot_in.reshape(cols_in, QUERIES, LQ),
            preferred_element_type=jnp.float32,
        )
        * weight[None]
    )
    sketch_part = jnp.einsum(
        "jr,qij->qri", test_matrix.astype(jnp.float32), moment, precision=highest
    )
    sketch = lax.psum(sketch_part, "docs")
    eig_wide = eig_out.astype(jnp.float32)
    gram_part = jnp.einsum("qri,qsi->qrs", sketch, sketch, precision=highest)
    gram_sum = lax.psum(gram_part, "basis")
    lower_factor = jnp.linalg.cholesky(gram_sum)
    range_rows = lax.linalg.triangular_solve(lower_factor, sketch, left_side=True, lower=True)
    proj_part = jnp.einsum("qri,qij->qrj", range_rows, moment, precision=highest)
    left_part = jnp.einsum("ia,qri->aqr", eig_wide, range_rows, precision=highest)
    projected, left_total = lax.psum((proj_part, left_part), "basis")
    left_sum = left_total.reshape(cols_out, QUERIES * RANK)
    projected_low = projected.astype(jnp.bfloat16).reshape(QUERIES * RANK, cols_in)
    right_part = lax.dot_general(
        eig_in, projected_low, (((1,), (1,)), ((), ())), preferred_element_type=jnp.float32
    )
    right_factor = lax.psum(right_part, "docs").astype(jnp.bfloat16)
    left_block = left_sum.astype(jnp.bfloat16)
    gathered = lax.all_gather(left_block, "docs", axis=0, tiled=True)
    rows_here = gradients.shape[1]
    left_local = lax.dynamic_slice_in_dim(
        gathered, lax.axis_index("basis") * rows_here, rows_here, 0
    )
    token_in, token_out = lax.psum(
        (
            jnp.dot(activations, right_factor, preferred_element_type=jnp.float32),
            jnp.dot(gradients, left_local, preferred_element_type=jnp.float32),
        ),
        "basis",
    )
    scores = (token_in * token_out).reshape(tok_count, QUERIES, RANK).sum(axis=2)
    positions = lax.axis_index("docs") * tok_count + jnp.arange(tok_count, dtype=jnp.int32)
    doc_ends = jnp.cumsum(doc_lengths)
    doc_starts = doc_ends - doc_lengths
    member = (
        (positions[:, None] >= doc_starts[None, :]) & (positions[:, None] < doc_ends[None, :])
    ).astype(jnp.float32)
    doc_part = lax.dot_general(member, scores, (((0,), (0,)), ((), ())), precision=highest)
    doc_influence = lax.psum(doc_part, "docs")
    return (scores, doc_influence)


def solution(mesh):
    return jax.shard_map(
        local,
        mesh=mesh,
        in_specs=(
            P("basis", "docs"),
            P("basis", "docs"),
            P("basis", "docs"),
            P("docs", None),
            P(("basis", "docs"), None),
            P("docs", None),
            P("docs", "basis"),
            P("docs", "basis"),
            P(),
        ),
        out_specs=(P("docs", None), P()),
        check_vma=False,
    )
```

profile of v0, /device:TPU:1, one launch (start us, length us, event | category | flops | bytes accessed | tf_op | source)
XLA Modules:
  0.0 913.8 jit_solution(15567339814722181471)
XLA Ops:
  7.2 40.4 %all_gather.6 = bf16[1792,256]{1,0:T(8,128)(2,1)S(1)} all-gather(bf16[56,256]{1,0:T(8,128)(2,1)} %param.13), channel_id=1, replica_groups=mesh['basis'=16,'docs'=32] {'docs'}, dimensions={0}, use_global_device_ids=true | all-gather | bytes 946176 | tf_op jit(solution)/shard_map/all_gather | solution.py:30
  47.7 2.0 fusion.22
  49.6 73.3 %all-reduce.12 = bf16[896,256]{1,0:T(8,128)(2,1)} all-reduce(f32[896,256]{1,0:T(8,128)} %fusion.22), channel_id=1, replica_groups=mesh['basis'=16,'docs'=32] {'basis'}, use_global_device_ids=true, to_apply=%region_1.0 | all-reduce | flops 229376 | bytes 1376256 | tf_op jit(solution)/shard_map/psum | solution.py:35
  123.0 2.0 copy.24
  125.0 1.9 fusion.21
  126.9 104.9 %all-reduce.13 = bf16[512,256]{1,0:T(8,128)(2,1)} all-reduce(f32[512,256]{1,0:T(8,128)} %fusion.21), channel_id=1, replica_groups=mesh['basis'=16,'docs'=32] {'docs'}, use_global_device_ids=true, to_apply=%region_0.0 | all-reduce | flops 131072 | bytes 786432 | tf_op jit(solution)/shard_map/psum | solution.py:36
  231.8 1.8 copy.23
  235.1 2.9 fusion.23
  237.9 3.0 copy-done.1
  240.9 4.8 fusion.6
  245.8 205.3 %all-reduce.9.cloned.1.call-done = f32[4,32,512]{2,1,0:T(8,128)} async-done(((f32[4,32,512]{2,1,0:T(8,128)}), f32[4,32,512]{2,1,0:T(8,128)}) %all-reduce.9.cloned.1.call-update) | async-done | bytes 262160 | tf_op jit(solution)/shard_map/psum | solution.py:50
  451.1 2.1 fusion.24
  453.2 61.2 %psum.73 = f32[4,32,32]{1,2,0:T(8,128)S(1)} all-reduce(f32[4,32,32]{1,2,0:T(8,128)} %fusion.24), channel_id=1, replica_groups=mesh['basis'=16,'docs'=32] {'basis'}, use_global_device_ids=true, to_apply=%region_3.0 | all-reduce | flops 4096 | bytes 32768 | tf_op jit(solution)/shard_map/psum | solution.py:53
  515.1 1.5 fusion.14
  516.5 12.4 %custom-call.7 = f32[4,32,32]{2,1,0:T(8,128)S(1)} custom-call(f32[4,32,32]{2,1,0:T(8,128)} %fusion.14), custom_call_target="Cholesky" | custom-call | tf_op jit(solution)/shard_map/jit(cholesky)/cholesky | solution.py:54
  529.8 10.5 %custom-call.8 = f32[4,1,32,32]{2,3,1,0:T(8,128)S(1)} custom-call(f32[4,1,32,32]{3,2,1,0:T(8,128)} %select_bitcast_fusion), custom_call_target="InvertDiagBlocksLowerTriangular" | custom-call | tf_op jit(solution)/shard_map/triangular_solve | solution.py:55
  541.7 7.3 fusion
  549.9 63.2 %all-reduce.14 = (bf16[4,32,896]{2,1,0:T(8,128)(2,1)S(1)}, bf16[256,4,32]{0,2,1:T(8,128)(2,1)}) all-reduce(f32[4,32,896]{2,1,0:T(8,128)} %fusion, f32[256,4,32]{0,2,1:T(8,128)} %convolution_bitcast_fusion.1), channel_id=1, replica_groups=mesh['basis'=16,'docs'=32] {'basis'}, use_global_device_ids=true, to_apply=%region_6.7 | all-reduce | flops 147456 | bytes 884736 | tf_op jit(solution)/shard_map/psum | solution.py:58
  613.2 1.9 convolution_bitcast_fusion
  615.2 125.7 %all-reduce.15 = bf16[1792,128]{0,1:T(8,128)(2,1)} all-reduce(f32[1792,128]{0,1:T(8,128)} %convolution_bitcast_fusion), channel_id=1, replica_groups=mesh['basis'=16,'docs'=32] {'docs'}, use_global_device_ids=true, to_apply=%region_7.8 | all-reduce | flops 229376 | bytes 1376256 | tf_op jit(solution)/shard_map/psum | solution.py:64
  740.8 2.1 convolution_bitcast_fusion.3
  742.9 1.8 convolution_bitcast_fusion.2
  745.1 111.6 %all-reduce.11.cloned.1.call-done = (f32[128,128]{0,1:T(8,128)}, f32[128,128]{0,1:T(8,128)}) async-done(((f32[128,128]{0,1:T(8,128)}, f32[128,128]{0,1:T(8,128)}), (f32[128,128]{0,1:T(8,128)}, f32[128,128]{0,1:T(8,128)})) %all-reduce.11.cloned.1.call-update) | async-done | bytes 131088 | tf_op jit(solution)/shard_map/psum | solution.py:71
  857.8 49.5 %psum.79 = f32[128,4]{0,1:T(4,128)} all-reduce(f32[128,4]{0,1:T(4,128)S(1)} %fusion.15), channel_id=1, replica_groups=mesh['basis'=16,'docs'=32] {'docs'}, use_global_device_ids=true, to_apply=%region_13.14 | all-reduce | flops 512 | bytes 4096 | tf_op jit(solution)/shard_map/psum | solution.py:86
  (36 shorter events, 7.0 us)
Async XLA Ops:
  7.2 40.5 %copy-start = (bf16[1792,896]{1,0:T(8,128)(2,1)S(1)}, bf16[1792,896]{1,0:T(8,128)(2,1)}, u32[]{:S(2)}) copy-start(bf16[1792,896]{1,0:T(8,128)(2,1)} %param.9) | copy-start | bytes 9633796
  7.2 444.0 %all-reduce.9.cloned.1.call-start = ((), (), s32[]{:S(2)}) async-start(), calls=%async_computation | async-start | bytes 524288 | tf_op jit(solution)/shard_map/psum | solution.py:50
  47.7 77.3 %copy-start.3 = (bf16[512,256]{1,0:T(8,128)(2,1)S(1)}, bf16[512,256]{1,0:T(8,128)(2,1)}, u32[]{:S(2)}) copy-start(bf16[512,256]{1,0:T(8,128)(2,1)} %param.10) | copy-start | bytes 786436
  235.0 2.9 copy-start.2
  235.0 5.9 copy-start.4
  237.9 3.0 copy-start.1
  245.7 497.1 %all-gather.2.cloned.1.call-start = ((), (), s32[]{:S(2)}) async-start(), calls=%async_computation.1 | async-start | bytes 2162688 | tf_op jit(solution)/shard_map/all_gather | solution.py:66
  613.1 243.5 %all-reduce.11.cloned.1.call-start = ((), (), s32[]{:S(2)}) async-start(), calls=%async_computation.2 | async-start | bytes 262144 | tf_op jit(solution)/shard_map/psum | solution.py:71
  613.2 131.5 %copy-start.6 = (s32[128]{0:T(128)S(1)}, s32[128]{0:T(128)}, u32[]{:S(2)}) copy-start(s32[128]{0:T(128)} %param.17) | copy-start | bytes 1540
  857.6 49.7 %copy-start.5 = (f32[128,4]{0,1:T(4,128)}, f32[128,4]{0,1:T(4,128)S(1)}, u32[]{:S(2)}) copy-start(f32[128,4]{0,1:T(4,128)S(1)} %bitcast_reduce_fusion) | copy-start | bytes 6148
Sparse Core Ops, SparseCore 0:
  245.9 205.2 all-reduce.8
  613.3 97.2 all-gather.1
  744.8 111.8 all-reduce.10
where the time goes:
time: 915 us; the launch traced here: 914 us
  blocking collectives  518 us (57%)
  waiting for transfers between devices  317 us (35%)
  matrix products  29.2 us (3%)
  other arithmetic  27.9 us (3%)
  between operations  13.9 us (2%)
    psum x1, waiting for transfers between devices, local(): sketch = lax.psum(sketch_part, 'docs')  205 us
    psum x1, blocking collectives, local(): right_factor = lax.psum(right_part, 'docs').astype(jnp.bfloat16)  126 us
    psum x1, waiting for transfers between devices, local(): lax.psum((jnp.dot(activations, right_factor, preferred_element_type=jnp.f...  112 us
    psum x1, blocking collectives, local(): rot_out = lax.psum(partial_out, 'docs').astype(jnp.bfloat16)  105 us
    psum x1, blocking collectives, local(): rot_in = lax.psum(partial_in, 'basis').astype(jnp.bfloat16)  73.3 us
    psum x1, blocking collectives, local(): projected, left_total = lax.psum((proj_part, left_part), 'basis')  63.2 us
    psum x1, blocking collectives, local(): gram_sum = lax.psum(gram_part, 'basis')  61.2 us
    psum x1, blocking collectives, local(): doc_influence = lax.psum(doc_part, 'docs')  49.5 us
  transfers between devices with their start and end apart: 3, of which 2 were waited for; matrix products, arithmetic and copies ran while one was open for 0% of the time, Pallas kernels for 0%

commit v1 on v0

--- a/solution.py
+++ b/solution.py
@@ -33,7 +33,7 @@
     )
     partial_out = jnp.dot(eig_out, out_factors, preferred_element_type=jnp.float32)
     rot_in = lax.psum(partial_in, "basis").astype(jnp.bfloat16)
-    rot_out = lax.psum(partial_out, "docs").astype(jnp.bfloat16)
+    rot_out = jnp.sum(lax.all_gather(partial_out, "docs"), axis=0).astype(jnp.bfloat16)
     weight = 1.0 / (eigvals.astype(jnp.float32) + damping)
     moment = (
         jnp.einsum(

time: 915 us -> 824 us (0.901)
  blocking collectives: 518 us -> 417 us
    psum x1 -> x0, blocking collectives: 105 us -> none  [local(): rot_out = lax.psum(partial_out, 'docs').astype(jnp.bfloat16)]
    psum x1, waiting for transfers between devices: 205 us -> 215 us  [local(): sketch = lax.psum(sketch_part, 'docs')]
  transfers between devices with their start and end apart: 3 -> 4, of which waited for: 2 -> 2; matrix products, arithmetic and copies ran while one was open for 0% -> 1% of each run, Pallas kernels for 0% -> 0%
where the time goes in v1:
time: 824 us; the launch traced here: 823 us
  blocking collectives  417 us (51%)
  waiting for transfers between devices  325 us (39%)
  other arithmetic  32.6 us (4%)
  matrix products  28.5 us (3%)
  between operations  13.9 us (2%)
    psum x1, waiting for transfers between devices, local(): sketch = lax.psum(sketch_part, 'docs')  215 us
    psum x1, blocking collectives, local(): right_factor = lax.psum(right_part, 'docs').astype(jnp.bfloat16)  127 us
    psum x1, waiting for transfers between devices, local(): lax.psum((jnp.dot(activations, right_factor, preferred_element_type=jnp.f...  110 us
    psum x1, blocking collectives, local(): rot_in = lax.psum(partial_in, 'basis').astype(jnp.bfloat16)  72.7 us
    psum x1, blocking collectives, local(): projected, left_total = lax.psum((proj_part, left_part), 'basis')  63.7 us
    psum x1, blocking collectives, local(): gram_sum = lax.psum(gram_part, 'basis')  60.6 us
    psum x1, blocking collectives, local(): doc_influence = lax.psum(doc_part, 'docs')  49.5 us
    all_gather x1, blocking collectives, local(): lax.all_gather(in_factors, 'docs', axis=0, tiled=True)  43 us
  transfers between devices with their start and end apart: 4, of which 2 were waited for; matrix products, arithmetic and copies ran while one was open for 1% of the time, Pallas kernels for 0%

profile of v1, /device:TPU:1, one launch (start us, length us, event | category | flops | bytes accessed | tf_op | source)
XLA Modules:
  0.0 823.4 jit_solution(6533426756541719198)
XLA Ops:
  7.2 2.2 fusion.21
  9.5 43.0 %all_gather.14 = bf16[1792,256]{1,0:T(8,128)(2,1)S(1)} all-gather(bf16[56,256]{1,0:T(8,128)(2,1)} %param.13), channel_id=1, replica_groups=mesh['basis'=16,'docs'=32] {'docs'}, dimensions={0}, use_global_device_ids=true | all-gather | bytes 946176 | tf_op jit(solution)/shard_map/all_gather | solution.py:30
  52.5 2.0 fusion.22
  54.5 72.7 %all-reduce.11 = bf16[896,256]{1,0:T(8,128)(2,1)} all-reduce(f32[896,256]{1,0:T(8,128)} %fusion.22), channel_id=1, replica_groups=mesh['basis'=16,'docs'=32] {'basis'}, use_global_device_ids=true, to_apply=%region_1.0 | all-reduce | flops 229376 | bytes 1376256 | tf_op jit(solution)/shard_map/psum | solution.py:35
  127.1 2.0 copy.34
  129.1 2.7 add_divide_fusion
  131.8 6.9 reduce_sum.18
  139.5 2.4 fusion.23
  141.9 3.0 copy-done.1
  144.9 4.8 fusion.6
  149.8 215.4 %all-reduce.8.cloned.1.call-done = f32[4,32,512]{2,1,0:T(8,128)} async-done(((f32[4,32,512]{2,1,0:T(8,128)}), f32[4,32,512]{2,1,0:T(8,128)}) %all-reduce.8.cloned.1.call-update) | async-done | bytes 262160 | tf_op jit(solution)/shard_map/psum | solution.py:50
  365.2 1.4 fusion.24
  366.6 60.6 %psum.65 = f32[4,32,32]{1,2,0:T(8,128)S(1)} all-reduce(f32[4,32,32]{1,2,0:T(8,128)S(1)} %fusion.24), channel_id=1, replica_groups=mesh['basis'=16,'docs'=32] {'basis'}, use_global_device_ids=true, to_apply=%region_3.0 | all-reduce | flops 4096 | bytes 32768 | tf_op jit(solution)/shard_map/psum | solution.py:53
  427.3 11.7 %custom-call.7 = f32[4,32,32]{2,1,0:T(8,128)S(1)} custom-call(f32[4,32,32]{2,1,0:T(8,128)S(1)} %fusion.14), custom_call_target="Cholesky" | custom-call | tf_op jit(solution)/shard_map/jit(cholesky)/cholesky | solution.py:54
  439.2 9.8 %custom-call.8 = f32[4,1,32,32]{2,3,1,0:T(8,128)S(1)} custom-call(f32[4,1,32,32]{3,2,1,0:T(8,128)S(1)} %select_bitcast_fusion), custom_call_target="InvertDiagBlocksLowerTriangular" | custom-call | tf_op jit(solution)/shard_map/triangular_solve | solution.py:55
  449.1 1.4 fusion.12
  450.5 7.3 fusion
  458.1 63.7 %all-reduce.12 = (bf16[4,32,896]{2,1,0:T(8,128)(2,1)}, bf16[256,4,32]{0,2,1:T(8,128)(2,1)}) all-reduce(f32[4,32,896]{2,1,0:T(8,128)} %fusion, f32[256,4,32]{0,2,1:T(8,128)S(1)} %convolution_bitcast_fusion.1), channel_id=1, replica_groups=mesh['basis'=16,'docs'=32] {'basis'}, use_global_device_ids=true, to_apply=%region_6.7 | all-reduce | flops 147456 | bytes 884736 | tf_op jit(solution)/shard_map/psum | solution.py:58
  521.9 2.9 convolution_bitcast_fusion
  524.8 127.5 %all-reduce.13 = bf16[1792,128]{0,1:T(8,128)(2,1)} all-reduce(f32[1792,128]{0,1:T(8,128)} %convolution_bitcast_fusion), channel_id=1, replica_groups=mesh['basis'=16,'docs'=32] {'docs'}, use_global_device_ids=true, to_apply=%region_7.8 | all-reduce | flops 229376 | bytes 1376256 | tf_op jit(solution)/shard_map/psum | solution.py:64
  652.2 2.1 convolution_bitcast_fusion.3
  654.3 1.7 convolution_bitcast_fusion.2
  656.5 109.8 %all-reduce.10.cloned.1.call-done = (f32[128,128]{0,1:T(8,128)}, f32[128,128]{0,1:T(8,128)}) async-done(((f32[128,128]{0,1:T(8,128)}, f32[128,128]{0,1:T(8,128)}), (f32[128,128]{0,1:T(8,128)}, f32[128,128]{0,1:T(8,128)})) %all-reduce.10.cloned.1.call-update) | async-done | bytes 131088 | tf_op jit(solution)/shard_map/psum | solution.py:71
  767.4 49.5 %psum.71 = f32[128,4]{0,1:T(4,128)} all-reduce(f32[128,4]{0,1:T(4,128)S(1)} %fusion.15), channel_id=1, replica_groups=mesh['basis'=16,'docs'=32] {'docs'}, use_global_device_ids=true, to_apply=%region_13.14 | all-reduce | flops 512 | bytes 4096 | tf_op jit(solution)/shard_map/psum | solution.py:86
  (41 shorter events, 3.2 us)
Async XLA Ops:
  7.2 45.3 %copy-start = (bf16[1792,896]{1,0:T(8,128)(2,1)S(1)}, bf16[1792,896]{1,0:T(8,128)(2,1)}, u32[]{:S(2)}) copy-start(bf16[1792,896]{1,0:T(8,128)(2,1)} %param.9) | copy-start | bytes 9633796
  7.2 124.6 %all-gather.6.cloned.1.call-start = ((), (), s32[]{:S(2)}) async-start(), calls=%async_computation.2 | async-start | bytes 17301504 | tf_op jit(solution)/shard_map/all_gather | solution.py:36
  9.4 355.8 %all-reduce.8.cloned.1.call-start = ((), (), s32[]{:S(2)}) async-start(), calls=%async_computation | async-start | bytes 524288 | tf_op jit(solution)/shard_map/psum | solution.py:50
  139.5 5.4 copy-start.2
  139.5 5.4 copy-start.5
  141.9 3.0 copy-start.1
  149.7 504.6 %all-gather.4.cloned.1.call-start = ((), (), s32[]{:S(2)}) async-start(), calls=%async_computation.1 | async-start | bytes 2162688 | tf_op jit(solution)/shard_map/all_gather | solution.py:66
  450.5 7.3 copy-start.3
  521.8 244.5 %all-reduce.10.cloned.1.call-start = ((), (), s32[]{:S(2)}) async-start(), calls=%async_computation.3 | async-start | bytes 262144 | tf_op jit(solution)/shard_map/psum | solution.py:71
  521.9 132.5 %copy-start.4 = (bf16[128,512]{1,0:T(8,128)(2,1)S(1)}, bf16[128,512]{1,0:T(8,128)(2,1)}, u32[]{:S(2)}) copy-start(bf16[128,512]{1,0:T(8,128)(2,1)} %param.16) | copy-start | bytes 393220
  521.9 134.2 %copy-start.7 = (s32[128]{0:T(128)S(1)}, s32[128]{0:T(128)}, u32[]{:S(2)}) copy-start(s32[128]{0:T(128)} %param.17) | copy-start | bytes 1540
  767.2 49.7 %copy-start.6 = (f32[128,4]{0,1:T(4,128)}, f32[128,4]{0,1:T(4,128)S(1)}, u32[]{:S(2)}) copy-start(f32[128,4]{0,1:T(4,128)S(1)} %bitcast_reduce_fusion) | copy-start | bytes 6148
Sparse Core Ops, SparseCore 0:
  10.1 114.5 all-gather.5
  149.8 215.3 all-reduce.7
  521.9 97.6 all-gather.3
  656.2 110.0 all-reduce.9
